TPU v7x, 32 devices: a whole 2x2x4 slice. The times are simulated.
32 devices in a mesh: groups: 2 (over x), ta: 16 (over z, y, core).
Axes of the slice: x: 2, y: 2, z: 4, core: 2. Of those that a mesh axis runs over, the one named last changes fastest.
Arguments:
- source: float32 [32, 4, 32, 256], P(('groups', 'ta')), parts along dimension 0, may hold values from -13 to 13
- links: float32 [16, 4, 9, 256, 256], P('ta'), may hold values from -0.046875 to 0.046875
- prolongator: float32 [16, 4, 16, 256], P('ta'), may hold values from -0.375 to 0.375
- coarse_inverse: float32 [1024, 1024], P('ta'), may hold values from -1 to 2
Outputs:
- solution: float32 [32, 4, 32, 256], P(('groups', 'ta')), parts along dimension 0
- residual: float32 [32, 4, 32, 256], P(('groups', 'ta')), parts along dimension 0
There are 2 independent parts, one for each index of `groups`. A program takes and returns all parts, laid end to end along the dimension named above; an argument that names none is the same for every part. Nothing has to cross between parts.
All inputs are finite; a program needn't handle non-finite values.
Results may differ from a plain program's by a relative error of at most 0.0003.
Values sent between devices are 32-bit elements; how exact they have to be, the bound alone decides.
A program may use at most 64 MiB of HBM per device.

v0:
```python
import jax
import jax.numpy as jnp
from jax import lax
from jax.sharding import PartitionSpec as P

LX = 1
LY = 2
LZ = 2
SWEEPS = 3
KS = 16


damping = 0.8
full_precision = lax.Precision.HIGHEST


def padded_2(cells, sides, width):
    for axis, dim in sides:
        count = lax.axis_size(axis)
        head = lax.slice_in_dim(cells, 0, width, axis=dim)
        tail = lax.slice_in_dim(cells, cells.shape[dim] - width, cells.shape[dim], axis=dim)
        cells = jnp.concatenate(
            [
                lax.ppermute(tail, axis, [(i, (i + 1) % count) for i in range(count)]),
                cells,
                lax.ppermute(head, axis, [((i + 1) % count, i) for i in range(count)]),
            ],
            axis=dim,
        )
    return cells


def neighbour_stack(padded):
    centre = padded[1:-1]
    shape = centre.shape
    grid = centre.reshape(shape[0], LX, LY, LZ, shape[2], shape[3])

    def rolled(amount, axis):
        return jnp.roll(grid, amount, axis).reshape(shape)

    return jnp.stack(
        [
            centre,
            padded[2:],
            padded[:-2],
            rolled(-1, 1),
            rolled(1, 1),
            rolled(-1, 2),
            rolled(1, 2),
            rolled(-1, 3),
            rolled(1, 3),
        ],
        axis=2,
    )


def operate(links, field):
    padded = padded_2(field, (("ta", 0),), 1)
    return field + jnp.einsum(
        "tsmab,tsmjb->tsja",
        links,
        neighbour_stack(padded),
        precision=full_precision,
        preferred_element_type=jnp.float32,
    )


def global_pair(image, residual):
    return lax.psum(
        (jnp.sum(image * residual, axis=(0, 1, 3)), jnp.sum(image * image, axis=(0, 1, 3))), "ta"
    )


def smooth(links, solution, residual):
    image = operate(links, residual)
    for sweep in range(SWEEPS):
        across, squared = global_pair(image, residual)
        if sweep + 1 < SWEEPS:
            further = operate(links, image)
        factor = (damping * across / squared)[:, None]
        solution = solution + factor * residual
        residual = residual - factor * image
        if sweep + 1 < SWEEPS:
            image = image - factor * further
    return (solution, residual)


def local(source, links, prolongator, coarse_inverse):
    slices = source.shape[0]
    sites = source.shape[1]
    columns = source.shape[2]
    unknowns = coarse_inverse.shape[0]
    solution = jnp.zeros_like(source)
    residual = source
    solution, residual = smooth(links, solution, residual)
    restricted = jnp.einsum(
        "tskc,tsjc->tskj",
        prolongator,
        residual,
        precision=full_precision,
        preferred_element_type=jnp.float32,
    ).reshape(unknowns, columns)
    coarse = jnp.dot(
        coarse_inverse,
        lax.all_gather(restricted, "ta", axis=0, tiled=True),
        precision=full_precision,
        preferred_element_type=jnp.float32,
    )
    correction = jnp.einsum(
        "tskc,tskj->tsjc",
        prolongator,
        coarse.reshape(slices, sites, KS, columns),
        precision=full_precision,
        preferred_element_type=jnp.float32,
    )
    image = operate(links, correction)
    across, squared = global_pair(image, residual)
    factor = (across / squared)[:, None]
    solution = solution + factor * correction
    residual = residual - factor * image
    solution, residual = smooth(links, solution, residual)
    return (solution, residual)


def solution(mesh):
    return jax.shard_map(
        local,
        mesh=mesh,
        in_specs=(
            P(("groups", "ta"), None, None, None),
            P("ta", None, None, None, None),
            P("ta", None, None, None),
            P("ta", None),
        ),
        out_specs=(P(("groups", "ta"), None, None, None), P(("groups", "ta"), None, None, None)),
        check_vma=False,
    )
```

profile of v0, /device:TPU:0, one launch (start us, length us, event | category | flops | bytes accessed | tf_op | source)
XLA Modules:
  0.0 355.7 jit_solution(11659418296701226594)
XLA Ops:
  0.7 5.5 %collective-permute-start = (f32[1,4,32,256]{3,2,1,0:T(8,128)}, f32[1,4,32,256]{3,2,1,0:T(8,128)S(1)}, u32[]{:S(2)}, u32[]{:S(2)}) collective-permute-start(f32[1,4,32,256]{3,2,1,0:T(8,128)} %param.4), channel_id=1, source_target_pairs={{1,0},{2,1},{3,2},{4,3},{5,4},{6,5},{7,6},{8,7},{9,8},{10,9},{11,1... | collective-permute-start | bytes 393224 | tf_op jit(solution)/shard_map/ppermute | solution.py:26
  6.2 0.9 constant_dynamic-update-slice_fusion.8
  7.1 0.9 fusion.149
  8.0 0.9 fusion.148
  9.0 0.1 collective-permute-done
  9.0 4.4 %collective-permute-done.1 = f32[1,4,32,256]{3,2,1,0:T(8,128)S(1)} collective-permute-done((f32[1,4,32,256]{3,2,1,0:T(8,128)}, f32[1,4,32,256]{3,2,1,0:T(8,128)S(1)}, u32[]{:S(2)}, u32[]{:S(2)}) %collective-permute-start.1) | collective-permute-done | bytes 131104 | tf_op jit(solution)/shard_map/ppermute | solution.py:24
  13.6 11.1 %constant_dynamic-update-slice_fusion.17 = (f32[1,4,9,32,256]{4,3,1,2,0:T(8,128)S(1)}, f32[1,4,32,256]{3,2,1,0:T(8,128)S(1)}) fusion(f32[1,4,32,256]{3,2,1,0:T(8,128)S(1)} %copy-done.1, f32[1,4,9,256,256]{4,3,2,1,0:T(8,128)} %param.5, f32[1,4,9,32,256]{4,3,2,1,0:T(8,128)S(1)} %constant_dynamic-update-slice_fusion), kind=kOutput, calls=%fused_computation.74 | convolution fusion | flops 906002432 | bytes 11010048 | tf_op jit(solution)/shard_map/tsmab,tsmjb->tsja/dot_general | solution.py:59
  24.7 0.1 collective-permute-start.2
  24.8 0.5 collective-permute-start.3
  25.3 0.1 multiply_reduce_fusion.12
  25.5 33.5 %all-reduce.6 = (f32[32]{0:T(128)S(1)}, f32[32]{0:T(128)S(1)}) all-reduce(f32[32]{0:T(128)S(1)} %get-tuple-element.13, f32[32]{0:T(128)S(1)} %get-tuple-element.12), channel_id=1, replica_groups=mesh['groups'=2,'ta'=16] {'ta'}, use_global_device_ids=true, to_apply=%region_3.4 | all-reduce | flops 64 | bytes 512 | tf_op jit(solution)/shard_map/psum | solution.py:69
  59.2 11.1 %constant_dynamic-update-slice_fusion.26 = (f32[1,4,9,32,256]{4,3,1,2,0:T(8,128)S(1)}, f32[1,4,32,256]{3,2,1,0:T(8,128)S(1)}) fusion(f32[1,4,32,256]{3,2,1,0:T(8,128)S(1)} %get-tuple-element.63, f32[1,4,9,32,256]{4,3,1,2,0:T(8,128)S(1)} %constant_dynamic-update-slice_fusion.9, f32[32]{0:T(128)S(1)} %multiply_divide_fusion.5, f32[1,4,9,256,256]{4,3,2,1,0:T(8,128)} %param.5), kind=kOutput, calls=%fused_computation.83 | convolution fusion | flops 906067968 | bytes 11010176 | tf_op jit(solution)/shard_map/tsmab,tsmjb->tsja/dot_general | solution.py:59
  70.3 0.2 multiply_reduce_fusion.10
  70.5 0.5 collective-permute-start.5
  71.1 33.7 %all-reduce.5 = (f32[32]{0:T(128)S(1)}, f32[32]{0:T(128)S(1)}) all-reduce(f32[32]{0:T(128)S(1)} %get-tuple-element.11, f32[32]{0:T(128)S(1)} %get-tuple-element.10), channel_id=1, replica_groups=mesh['groups'=2,'ta'=16] {'ta'}, use_global_device_ids=true, to_apply=%region_7.8 | all-reduce | flops 64 | bytes 512 | tf_op jit(solution)/shard_map/psum | solution.py:69
  105.0 11.3 %multiply_reduce_fusion.8 = (f32[32]{0:T(128)S(1)}, f32[32]{0:T(128)S(1)}, f32[1,4,32,256]{3,2,1,0:T(8,128)S(1)}) fusion(f32[1,4,32,256]{3,2,1,0:T(8,128)S(1)} %get-tuple-element.31, f32[1,4,32,256]{3,2,1,0:T(8,128)S(1)} %get-tuple-element.65, f32[32]{0:T(128)S(1)} %multiply_divide_fusion.4, ...), kind=kOutput, calls=%fused_computation.141 | convolution fusion | flops 906264512 | bytes 11010432 | tf_op jit(solution)/shard_map/tsmab,tsmjb->tsja/dot_general | solution.py:59
  116.2 29.5 %all-reduce.4 = (f32[32]{0:T(128)S(1)}, f32[32]{0:T(128)S(1)}) all-reduce(f32[32]{0:T(128)S(1)} %get-tuple-element.9, f32[32]{0:T(128)S(1)} %get-tuple-element.8), channel_id=1, replica_groups=mesh['groups'=2,'ta'=16] {'ta'}, use_global_device_ids=true, to_apply=%region_11.12 | all-reduce | flops 64 | bytes 512 | tf_op jit(solution)/shard_map/psum | solution.py:69
  145.7 0.1 multiply_subtract_fusion.3
  145.8 0.2 fusion.130
  146.1 0.1 copy.30
  146.1 17.9 %all-gather = f32[16,64,32]{1,2,0:T(8,128)S(1)} all-gather(f32[1,64,32]{1,2,0:T(8,128)S(1)} %copy.30), channel_id=1, replica_groups=mesh['groups'=2,'ta'=16] {'ta'}, dimensions={0}, use_global_device_ids=true | all-gather | bytes 139264 | tf_op jit(solution)/shard_map/all_gather | solution.py:105
  164.0 0.2 copy.31
  164.2 0.1 reshape.135
  164.3 0.3 convolution_bitcast_fusion
  164.6 0.1 copy.32
  164.7 0.3 constant_dynamic-update-slice_fusion.35
  165.1 2.1 collective-permute-start.6
  167.2 2.4 collective-permute-done.6
  169.7 4.6 %collective-permute-done.7 = f32[1,4,32,256]{3,2,1,0:T(8,128)S(1)} collective-permute-done((f32[1,4,32,256]{3,2,1,0:T(8,128)S(1)}, f32[1,4,32,256]{3,2,1,0:T(8,128)S(1)}, u32[]{:S(2)}, u32[]{:S(2)}) %collective-permute-start.7) | collective-permute-done | bytes 131104 | tf_op jit(solution)/shard_map/ppermute | solution.py:24
  174.4 11.2 %fusion.129 = (f32[32]{0:T(128)S(1)}, f32[4,32,256]{2,1,0:T(8,128)S(1)}) fusion(f32[1,4,32,256]{3,2,1,0:T(8,128)S(1)} %multiply_subtract_fusion.3, f32[4,32,256]{2,1,0:T(8,128)S(1)} %get-tuple-element.68, f32[1,4,9,32,256]{4,3,1,2,0:T(8,128)S(1)} %constant_dynamic-update-slice_fusion.27, f32[1,4,9,256,256]{4,3,2,1,0:T(8,128)} %param.5), kind=kOutput, calls=%fused_computation.126 | convolution fusion | flops 906067968 | bytes 11010176 | tf_op jit(solution)/shard_map/tsmab,tsmjb->tsja/dot_general | solution.py:59
  185.6 0.1 multiply_reduce_fusion.6
  185.8 29.5 %all-reduce.3 = (f32[32]{0:T(128)S(1)}, f32[32]{0:T(128)S(1)}) all-reduce(f32[32]{0:T(128)S(1)} %get-tuple-element.69, f32[32]{0:T(128)S(1)} %multiply_reduce_fusion.6), channel_id=1, replica_groups=mesh['groups'=2,'ta'=16] {'ta'}, use_global_device_ids=true, to_apply=%region_13.14 | all-reduce | flops 64 | bytes 512 | tf_op jit(solution)/shard_map/psum | solution.py:69
  215.3 0.1 constant_dynamic-update-slice_fusion.44
  215.4 0.1 collective-permute-start.8
  215.4 0.5 collective-permute-start.9
  216.0 1.9 collective-permute-done.8
  218.0 4.8 %collective-permute-done.9 = f32[1,4,32,256]{3,2,1,0:T(8,128)S(1)} collective-permute-done((f32[1,4,32,256]{3,2,1,0:T(8,128)S(1)}, f32[1,4,32,256]{3,2,1,0:T(8,128)S(1)}, u32[]{:S(2)}, u32[]{:S(2)}) %collective-permute-start.9) | collective-permute-done | bytes 131104 | tf_op jit(solution)/shard_map/ppermute | solution.py:24
  222.9 11.1 %constant_dynamic-update-slice_fusion.53 = (f32[1,4,9,32,256]{4,3,1,2,0:T(8,128)S(1)}, f32[1,4,32,256]{3,2,1,0:T(8,128)S(1)}) fusion(f32[1,4,32,256]{3,2,1,0:T(8,128)S(1)} %get-tuple-element.30, f32[1,4,9,32,256]{4,3,1,2,0:T(8,128)S(1)} %constant_dynamic-update-slice_fusion.36, f32[1,4,9,256,256]{4,3,2,1,0:T(8,128)} %param.5), kind=kOutput, calls=%fused_computation.110 | convolution fusion | flops 906002432 | bytes 11010048 | tf_op jit(solution)/shard_map/tsmab,tsmjb->tsja/dot_general | solution.py:59
  234.1 0.5 collective-permute-start.11
  234.6 0.1 multiply_reduce_fusion.5
  234.8 33.5 %all-reduce.2 = (f32[32]{0:T(128)S(1)}, f32[32]{0:T(128)S(1)}) all-reduce(f32[32]{0:T(128)S(1)} %get-tuple-element.7, f32[32]{0:T(128)S(1)} %get-tuple-element.6), channel_id=1, replica_groups=mesh['groups'=2,'ta'=16] {'ta'}, use_global_device_ids=true, to_apply=%region_19.20 | all-reduce | flops 64 | bytes 512 | tf_op jit(solution)/shard_map/psum | solution.py:69
  268.5 11.1 %constant_dynamic-update-slice_fusion.62 = (f32[1,4,9,32,256]{4,3,1,2,0:T(8,128)S(1)}, f32[1,4,32,256]{3,2,1,0:T(8,128)S(1)}) fusion(f32[1,4,32,256]{3,2,1,0:T(8,128)S(1)} %get-tuple-element.72, f32[1,4,9,32,256]{4,3,1,2,0:T(8,128)S(1)} %constant_dynamic-update-slice_fusion.45, f32[32]{0:T(128)S(1)} %multiply_divide_fusion.2, f32[1,4,9,256,256]{4,3,2,1,0:T(8,128)} %param.5), kind=kOutput, calls=%fused_computation.119 | convolution fusion | flops 906067968 | bytes 11010176 | tf_op jit(solution)/shard_map/tsmab,tsmjb->tsja/dot_general | solution.py:59
  279.6 0.2 multiply_reduce_fusion.3
  279.8 0.5 collective-permute-start.13
  280.4 33.5 %all-reduce.1 = (f32[32]{0:T(128)S(1)}, f32[32]{0:T(128)S(1)}) all-reduce(f32[32]{0:T(128)S(1)} %get-tuple-element.5, f32[32]{0:T(128)S(1)} %get-tuple-element.4), channel_id=1, replica_groups=mesh['groups'=2,'ta'=16] {'ta'}, use_global_device_ids=true, to_apply=%region_23.24 | all-reduce | flops 64 | bytes 512 | tf_op jit(solution)/shard_map/psum | solution.py:69
  314.1 11.2 %multiply_reduce_fusion.1 = (f32[32]{0:T(128)S(1)}, f32[32]{0:T(128)S(1)}, f32[1,4,32,256]{3,2,1,0:T(8,128)S(1)}) fusion(f32[1,4,32,256]{3,2,1,0:T(8,128)S(1)} %get-tuple-element.28, f32[1,4,32,256]{3,2,1,0:T(8,128)S(1)} %get-tuple-element.74, f32[32]{0:T(128)S(1)} %multiply_divide_fusion.1, ...), kind=kOutput, calls=%fused_computation.131 | convolution fusion | flops 906264512 | bytes 11010432 | tf_op jit(solution)/shard_map/tsmab,tsmjb->tsja/dot_general | solution.py:59
  325.3 29.5 %all-reduce = (f32[32]{0:T(128)S(1)}, f32[32]{0:T(128)S(1)}) all-reduce(f32[32]{0:T(128)S(1)} %get-tuple-element.3, f32[32]{0:T(128)S(1)} %get-tuple-element.2), channel_id=1, replica_groups=mesh['groups'=2,'ta'=16] {'ta'}, use_global_device_ids=true, to_apply=%region_27.28 | all-reduce | flops 64 | bytes 512 | tf_op jit(solution)/shard_map/psum | solution.py:69
  354.8 0.9 multiply_subtract_fusion
  (112 shorter events, 1.2 us)
Async XLA Ops:
  0.6 163.7 %copy-start = (f32[64,1024]{1,0:T(8,128)S(1)}, f32[64,1024]{1,0:T(8,128)}, u32[]{:S(2)}) copy-start(f32[64,1024]{1,0:T(8,128)} %param.7) | copy-start | bytes 786436
  0.6 12.9 %copy-start.1 = (f32[1,4,32,256]{3,2,1,0:T(8,128)S(1)}, f32[1,4,32,256]{3,2,1,0:T(8,128)}, u32[]{:S(2)}) copy-start(f32[1,4,32,256]{3,2,1,0:T(8,128)} %param.4) | copy-start | bytes 393220
  0.7 8.4 %collective-permute-start = (f32[1,4,32,256]{3,2,1,0:T(8,128)}, f32[1,4,32,256]{3,2,1,0:T(8,128)S(1)}, u32[]{:S(2)}, u32[]{:S(2)}) collective-permute-start(f32[1,4,32,256]{3,2,1,0:T(8,128)} %param.4), channel_id=1, source_target_pairs={{1,0},{2,1},{3,2},{4,3},{5,4},{6,5},{7,6},{8,7},{9,8},{10,9},{11,1... | collective-permute-start | bytes 393224 | tf_op jit(solution)/shard_map/ppermute | solution.py:26
  6.2 7.3 %collective-permute-start.1 = (f32[1,4,32,256]{3,2,1,0:T(8,128)}, f32[1,4,32,256]{3,2,1,0:T(8,128)S(1)}, u32[]{:S(2)}, u32[]{:S(2)}) collective-permute-start(f32[1,4,32,256]{3,2,1,0:T(8,128)} %param.4), channel_id=1, source_target_pairs={{0,1},{1,2},{2,3},{3,4},{4,5},{5,6},{6,7},{7,8},{8,9},{9,10},{10,1... | collective-permute-start | bytes 393224 | tf_op jit(solution)/shard_map/ppermute | solution.py:24
  24.7 34.2 %collective-permute-start.2 = (f32[1,4,32,256]{3,2,1,0:T(8,128)S(1)}, f32[1,4,32,256]{3,2,1,0:T(8,128)S(1)}, u32[]{:S(2)}, u32[]{:S(2)}) collective-permute-start(f32[1,4,32,256]{3,2,1,0:T(8,128)S(1)} %get-tuple-element.63), channel_id=1, source_target_pairs={{1,0},{2,1},{3,2},{4,3},{5,4},{6,5},{7,6},{8,7},{9,8},{10,9},{11,1... | collective-permute-start | bytes 393224 | tf_op jit(solution)/shard_map/ppermute | solution.py:26
  24.8 34.2 %collective-permute-start.3 = (f32[1,4,32,256]{3,2,1,0:T(8,128)S(1)}, f32[1,4,32,256]{3,2,1,0:T(8,128)S(1)}, u32[]{:S(2)}, u32[]{:S(2)}) collective-permute-start(f32[1,4,32,256]{3,2,1,0:T(8,128)S(1)} %get-tuple-element.63), channel_id=1, source_target_pairs={{0,1},{1,2},{2,3},{3,4},{4,5},{5,6},{6,7},{7,8},{8,9},{9,10},{10,1... | collective-permute-start | bytes 393224 | tf_op jit(solution)/shard_map/ppermute | solution.py:24
  70.5 34.3 %collective-permute-start.4 = (f32[1,4,32,256]{3,2,1,0:T(8,128)S(1)}, f32[1,4,32,256]{3,2,1,0:T(8,128)S(1)}, u32[]{:S(2)}, u32[]{:S(2)}) collective-permute-start(f32[1,4,32,256]{3,2,1,0:T(8,128)S(1)} %get-tuple-element.65), channel_id=1, source_target_pairs={{1,0},{2,1},{3,2},{4,3},{5,4},{6,5},{7,6},{8,7},{9,8},{10,9},{11,1... | collective-permute-start | bytes 393224 | tf_op jit(solution)/shard_map/ppermute | solution.py:26
  70.5 34.3 %collective-permute-start.5 = (f32[1,4,32,256]{3,2,1,0:T(8,128)S(1)}, f32[1,4,32,256]{3,2,1,0:T(8,128)S(1)}, u32[]{:S(2)}, u32[]{:S(2)}) collective-permute-start(f32[1,4,32,256]{3,2,1,0:T(8,128)S(1)} %get-tuple-element.65), channel_id=1, source_target_pairs={{0,1},{1,2},{2,3},{3,4},{4,5},{5,6},{6,7},{7,8},{8,9},{9,10},{10,1... | collective-permute-start | bytes 393224 | tf_op jit(solution)/shard_map/ppermute | solution.py:24
  104.9 40.9 %copy-start.2 = (f32[1,4,16,256]{3,2,1,0:T(8,128)S(1)}, f32[1,4,16,256]{3,2,1,0:T(8,128)}, u32[]{:S(2)}) copy-start(f32[1,4,16,256]{3,2,1,0:T(8,128)} %param.6) | copy-start | bytes 196612
  145.7 18.9 %copy-start.3 = (f32[32]{0:T(128)}, f32[32]{0:T(128)S(1)}, u32[]{:S(2)}) copy-start(f32[32]{0:T(128)S(1)} %multiply_divide_fusion.3) | copy-start | bytes 388
  165.1 4.6 %collective-permute-start.6 = (f32[1,4,32,256]{3,2,1,0:T(8,128)S(1)}, f32[1,4,32,256]{3,2,1,0:T(8,128)S(1)}, u32[]{:S(2)}, u32[]{:S(2)}) collective-permute-start(f32[1,4,32,256]{3,2,1,0:T(8,128)S(1)} %bitcast.279), channel_id=1, source_target_pairs={{1,0},{2,1},{3,2},{4,3},{5,4},{6,5},{7,6},{8,7},{9,8},{10,9},{11,1... | collective-permute-start | bytes 393224 | tf_op jit(solution)/shard_map/ppermute | solution.py:26
  167.2 7.1 %collective-permute-start.7 = (f32[1,4,32,256]{3,2,1,0:T(8,128)S(1)}, f32[1,4,32,256]{3,2,1,0:T(8,128)S(1)}, u32[]{:S(2)}, u32[]{:S(2)}) collective-permute-start(f32[1,4,32,256]{3,2,1,0:T(8,128)S(1)} %bitcast.280), channel_id=1, source_target_pairs={{0,1},{1,2},{2,3},{3,4},{4,5},{5,6},{6,7},{7,8},{8,9},{9,10},{10,1... | collective-permute-start | bytes 393224 | tf_op jit(solution)/shard_map/ppermute | solution.py:24
  215.4 2.6 collective-permute-start.8
  215.4 7.4 %collective-permute-start.9 = (f32[1,4,32,256]{3,2,1,0:T(8,128)S(1)}, f32[1,4,32,256]{3,2,1,0:T(8,128)S(1)}, u32[]{:S(2)}, u32[]{:S(2)}) collective-permute-start(f32[1,4,32,256]{3,2,1,0:T(8,128)S(1)} %get-tuple-element.30), channel_id=1, source_target_pairs={{0,1},{1,2},{2,3},{3,4},{4,5},{5,6},{6,7},{7,8},{8,9},{9,10},{10,1... | collective-permute-start | bytes 393224 | tf_op jit(solution)/shard_map/ppermute | solution.py:24
  234.0 34.2 %collective-permute-start.10 = (f32[1,4,32,256]{3,2,1,0:T(8,128)S(1)}, f32[1,4,32,256]{3,2,1,0:T(8,128)S(1)}, u32[]{:S(2)}, u32[]{:S(2)}) collective-permute-start(f32[1,4,32,256]{3,2,1,0:T(8,128)S(1)} %get-tuple-element.72), channel_id=1, source_target_pairs={{1,0},{2,1},{3,2},{4,3},{5,4},{6,5},{7,6},{8,7},{9,8},{10,9},{11,1... | collective-permute-start | bytes 393224 | tf_op jit(solution)/shard_map/ppermute | solution.py:26
  234.1 34.2 %collective-permute-start.11 = (f32[1,4,32,256]{3,2,1,0:T(8,128)S(1)}, f32[1,4,32,256]{3,2,1,0:T(8,128)S(1)}, u32[]{:S(2)}, u32[]{:S(2)}) collective-permute-start(f32[1,4,32,256]{3,2,1,0:T(8,128)S(1)} %get-tuple-element.72), channel_id=1, source_target_pairs={{0,1},{1,2},{2,3},{3,4},{4,5},{5,6},{6,7},{7,8},{8,9},{9,10},{10,1... | collective-permute-start | bytes 393224 | tf_op jit(solution)/shard_map/ppermute | solution.py:24
  279.8 34.1 %collective-permute-start.12 = (f32[1,4,32,256]{3,2,1,0:T(8,128)S(1)}, f32[1,4,32,256]{3,2,1,0:T(8,128)S(1)}, u32[]{:S(2)}, u32[]{:S(2)}) collective-permute-start(f32[1,4,32,256]{3,2,1,0:T(8,128)S(1)} %get-tuple-element.74), channel_id=1, source_target_pairs={{1,0},{2,1},{3,2},{4,3},{5,4},{6,5},{7,6},{8,7},{9,8},{10,9},{11,1... | collective-permute-start | bytes 393224 | tf_op jit(solution)/shard_map/ppermute | solution.py:26
  279.8 34.1 %collective-permute-start.13 = (f32[1,4,32,256]{3,2,1,0:T(8,128)S(1)}, f32[1,4,32,256]{3,2,1,0:T(8,128)S(1)}, u32[]{:S(2)}, u32[]{:S(2)}) collective-permute-start(f32[1,4,32,256]{3,2,1,0:T(8,128)S(1)} %get-tuple-element.74), channel_id=1, source_target_pairs={{0,1},{1,2},{2,3},{3,4},{4,5},{5,6},{6,7},{7,8},{8,9},{9,10},{10,1... | collective-permute-start | bytes 393224 | tf_op jit(solution)/shard_map/ppermute | solution.py:24
  314.1 40.8 %copy-start.4 = (f32[32]{0:T(128)S(1)}, f32[32]{0:T(128)}, u32[]{:S(2)}) copy-start(f32[32]{0:T(128)} %copy-done.3) | copy-start | bytes 388
where the time goes:
time: 356 us
  blocking collectives  240 us (67%)
  matrix products  79.1 us (22%)
  waiting for transfers between devices  18.3 us (5%)
  starting transfers between devices  10.4 us (3%)
  local copies, waits for them, and re-layouts  3.94 us (1%)
    psum x7, blocking collectives, global_pair(): lax.psum((jnp.sum(image * residual, axis=(0, 1, 3)), jnp.sum(image * imag...  223 us
    dot_general x7, matrix products, operate(): jnp.einsum('tsmab,tsmjb->tsja', links, neighbour_stack(padded), precision...  78.2 us
    all_gather x1, blocking collectives, local(): lax.all_gather(restricted, 'ta', axis=0, tiled=True)  17.9 us
    ppermute x7, waiting for transfers between devices, padded_2(): lax.ppermute(tail, axis, [(i, (i + 1) % count) for i in range(count)])  13.8 us
    ppermute x7, starting transfers between devices, padded_2(): lax.ppermute(head, axis, [((i + 1) % count, i) for i in range(count)])  7.94 us
  transfers between devices with their start and end apart: 14, of which 6 were waited for; matrix products, arithmetic and copies ran while one was open for 1% of the time, Pallas kernels for 0%

commit v1 on v0

v1 whole, which is shorter than its diff:
```python
import functools

import jax
import jax.numpy as jnp
from jax import lax
from jax.experimental import pallas as pl
from jax.experimental.pallas import tpu as pltpu
from jax.sharding import PartitionSpec as P

LINK_SUMS = ((0, 3, 4), (5, 6), (7, 8), (1,), (2,))
INNER_SUMS = 3
DAMPING = 0.8
SWEEPS = 3
STEP = 0.8
HIGHEST = lax.Precision.HIGHEST
F32 = jnp.float32
BF16 = jnp.bfloat16
GRAM_ROWS = 8


def dot(a, b):
    return jnp.dot(a, b, precision=HIGHEST, preferred_element_type=F32)


def kernel(
    n,
    source_ref,
    links_ref,
    prol_ref,
    inverse_ref,
    solution_ref,
    residual_ref,
    raw,
    lcat,
    weights,
    field,
    halo,
    acc,
    stage,
    gather,
    small_stage,
    small,
    rall,
    link_sem,
    halo_send,
    halo_recv,
    gather_send,
    gather_recv,
    small_send,
    small_recv,
):
    me = lax.axis_index("ta")
    sites, rhs, comps = source_ref.shape[1:]
    ks = prol_ref.shape[2]
    width = sites * rhs
    right, left = lax.rem(me + 1, n), lax.rem(me + n - 1, n)

    barrier = pltpu.get_barrier_semaphore()

    def greet(d, carry):
        pl.semaphore_signal(barrier, inc=1, device_id={"ta": lax.rem(me + d, n)})
        return carry

    lax.fori_loop(1, n, greet, 0)
    for s in range(sites):
        pltpu.make_async_copy(links_ref.at[0, s], raw.at[s], link_sem.at[s]).start()

    lane_site = lax.broadcasted_iota(jnp.int32, (1, width), 1) // rhs
    even = lane_site % 2 == 0

    def over_sites(x):
        shift = rhs
        while shift < width:
            x = x + pltpu.roll(x, shift, 1)
            shift *= 2
        return x

    prol = prol_ref[0].reshape(sites * ks, comps)
    row_site = lax.broadcasted_iota(jnp.int32, (sites * ks, width), 0) // ks
    diagonal = row_site == lax.broadcasted_iota(jnp.int32, (sites * ks, width), 1) // rhs

    def restrict(v):
        full = jnp.where(diagonal, dot(prol, v), 0.0)
        return functools.reduce(jnp.add, [full[s * ks : (s + 1) * ks] for s in range(sites)])

    def products(pairs):
        rows = [jnp.sum(a * b, axis=0, keepdims=True) for a, b in pairs]
        return jnp.concatenate(rows + [jnp.zeros((GRAM_ROWS - len(rows), width), F32)], axis=0)

    def halo_copies(r, f):
        out = []
        for side, to in ((0, left), (1, right)):
            out.append(
                pltpu.make_async_remote_copy(
                    src_ref=field.at[f],
                    dst_ref=halo.at[r, side],
                    send_sem=halo_send.at[r, side],
                    recv_sem=halo_recv.at[r, side],
                    device_id={"ta": to},
                )
            )
        return out

    sent = []

    def send_halo(r, f):
        copies = halo_copies(r, f)
        for c in copies:
            c.start()
        sent.extend(copies)
        return copies

    def exchange(k, value, staged, slots, send_sem, recv_sem):
        staged[k] = value
        slots[k, me] = value

        def one(d, carry):
            pltpu.make_async_remote_copy(
                src_ref=staged.at[k],
                dst_ref=slots.at[k, me],
                send_sem=send_sem.at[k],
                recv_sem=recv_sem.at[k],
                device_id={"ta": lax.rem(me + d, n)},
            ).start()
            return carry

        lax.fori_loop(1, n, one, 0)
        return pltpu.make_async_remote_copy(
            src_ref=slots.at[k, pl.ds(0, n - 1)],
            dst_ref=slots.at[k, pl.ds(0, n - 1)],
            send_sem=send_sem.at[k],
            recv_sem=recv_sem.at[k],
            device_id={"ta": right},
        )

    pending = []

    def exchange_large(k, value):
        c = exchange(k, value, stage, gather, gather_send, gather_recv)
        pending.append(c)
        return c

    def exchange_small(k, value):
        c = exchange(k, value, small_stage, small, small_send, small_recv)
        pending.append(c)
        return c

    def load_weights(at, v):
        hi = v.astype(BF16)
        lo = (v - hi.astype(F32)).astype(BF16)
        weights[at * comps : (at + 1) * comps, :width] = hi
        weights[at * comps : (at + 1) * comps, width:] = lo

    def multiply(lo_k, hi_k, add):
        def site(s, carry):
            p = jnp.dot(
                lcat[s, :, lo_k * comps : hi_k * comps],
                weights[lo_k * comps : hi_k * comps],
                preferred_element_type=F32,
            )
            z = p[:comps, :width] + p[:comps, width:] + p[comps:, :width]
            if add:
                acc[...] += jnp.where(lane_site == s, z, 0.0)
            else:
                acc[...] = jnp.where(lane_site == s, z, acc[...])
            return carry

        lax.fori_loop(0, sites, site, 0)

    def hop(r, f, shade=None):
        v = field[f]
        load_weights(0, v)
        load_weights(1, pltpu.roll(v, width // 2, 1))
        load_weights(2, jnp.where(even, pltpu.roll(v, width - rhs, 1), pltpu.roll(v, rhs, 1)))
        multiply(0, INNER_SUMS, False)
        copies = sent[-2:]
        for side, c in enumerate(copies):
            c.wait_recv()
            load_weights(INNER_SUMS + side, halo[r, side])
        multiply(INNER_SUMS, len(LINK_SUMS), True)
        return acc[...]

    def step(r, f, to):
        field[to] = (1.0 - STEP) * field[f] - STEP * hop(r, f)

    def sweeps(gram):
        c = [jnp.ones((1, width), F32)]
        x = [jnp.zeros((1, width), F32)] * SWEEPS
        for _ in range(SWEEPS):
            size = len(c)
            d = [(c[0]) / STEP] + [(c[i] - c[i - 1]) / STEP for i in range(1, size)] + [-c[-1] / STEP]
            gd = [
                functools.reduce(jnp.add, [gram(i, j) * d[j] for j in range(size + 1)])
                for i in range(size + 1)
            ]
            across = functools.reduce(jnp.add, [gd[i] * c[i] for i in range(size)])
            squared = functools.reduce(jnp.add, [gd[i] * d[i] for i in range(size + 1)])
            factor = DAMPING * across / squared
            x = [x[i] + factor * c[i] if i < size else x[i] for i in range(SWEEPS)]
            c = [c[i] - factor * d[i] if i < size else -factor * d[i] for i in range(size + 1)]
        return c, x

    def combine(coefficients, fields):
        return functools.reduce(jnp.add, [a * field[f] for a, f in zip(coefficients, fields)])

    field[0] = source_ref[0].reshape(width, comps).T
    pl.semaphore_wait(barrier, n - 1)
    send_halo(0, 0)

    def prepare(s, carry):
        pltpu.make_async_copy(links_ref.at[0, s], raw.at[s], link_sem.at[s]).wait()
        for at, members in enumerate(LINK_SUMS):
            total = functools.reduce(jnp.add, [raw[s, m] for m in members])
            hi = total.astype(BF16)
            lo = (total - hi.astype(F32)).astype(BF16)
            lcat[s, :comps, at * comps : (at + 1) * comps] = hi
            lcat[s, comps:, at * comps : (at + 1) * comps] = lo
        return carry

    lax.fori_loop(0, sites, prepare, 0)
    for k in range(SWEEPS + 1):
        if k:
            send_halo(k, k)
        value = jnp.concatenate(
            [restrict(field[k]), products([(field[k], field[i]) for i in range(k + 1)])], axis=0
        )
        exchange_large(k, value)
        step(k, k, k + 1)
    for k in range(SWEEPS + 1):
        pending[k].wait_recv()

    def total_of(slots, k, at):
        def one(t, total):
            return total + slots[k, t, at : at + GRAM_ROWS]

        return over_sites(lax.fori_loop(0, n, one, jnp.zeros((GRAM_ROWS, width), F32)))

    grams = [total_of(gather, k, ks) for k in range(SWEEPS + 1)]
    c, x = sweeps(lambda i, j: grams[max(i, j)][min(i, j) : min(i, j) + 1])

    def spread(t, carry):
        r = functools.reduce(jnp.add, [c[k] * gather[k, t, :ks] for k in range(SWEEPS + 1)])
        for s in range(sites):
            rall[pl.ds(pl.multiple_of((t * sites + s) * ks, ks), ks)] = jnp.where(
                lane_site == s, r, 0.0
            )
        return carry

    lax.fori_loop(0, n, spread, 0)
    coarse = over_sites(dot(inverse_ref[...], rall[...]))
    field[5] = dot(prol.T, jnp.where(diagonal, coarse, 0.0))
    send_halo(4, 5)
    residual = combine(c, range(SWEEPS + 1))
    field[7] = residual
    field[8] = combine(c, range(1, SWEEPS + 2))
    field[9] = combine(x, range(SWEEPS))
    field[6] = field[5] + hop(4, 5)
    send_halo(5, 6)
    exchange_small(0, products([(field[6], field[7]), (field[6], field[6])]))
    after = (1.0 - STEP) * field[6] - STEP * hop(5, 6)
    pending[-1].wait_recv()
    pair = total_of(small, 0, 0)
    g = pair[0:1] / pair[1:2]

    field[11] = field[8] - g * after
    send_halo(6, 11)
    field[10] = field[7] - g * field[6]
    field[9] = field[9] + g * field[5]
    step(6, 11, 12)
    send_halo(7, 12)
    early = [(i, j) for i in range(3) for j in range(i + 1)]
    late = [(3, j) for j in range(4)]
    exchange_small(1, products([(field[10 + i], field[10 + j]) for i, j in early]))
    step(7, 12, 13)
    exchange_small(2, products([(field[10 + i], field[10 + j]) for i, j in late]))
    pending[-2].wait_recv()
    pending[-1].wait_recv()
    sums = [total_of(small, 1, 0), total_of(small, 2, 0)]

    def gram(i, j):
        pair = (max(i, j), min(i, j))
        which = 0 if pair in early else 1
        row = (early, late)[which].index(pair)
        return sums[which][row : row + 1]

    c, x = sweeps(gram)
    residual_ref[0] = combine(c, range(10, 14)).T.reshape(sites, rhs, comps)
    solution_ref[0] = (field[9] + combine(x, range(10, 13))).T.reshape(sites, rhs, comps)
    for copy in sent + pending:
        copy.wait_send()


def local(source, links, prolongator, coarse_inverse):
    n = lax.axis_size("ta")
    _, sites, rhs, comps = source.shape
    ks = prolongator.shape[2]
    width = sites * rhs
    sums = len(LINK_SUMS)
    vmem = pl.BlockSpec(memory_space=pltpu.VMEM)
    dma = pltpu.SemaphoreType.DMA
    return pl.pallas_call(
        functools.partial(kernel, n),
        out_shape=(jax.ShapeDtypeStruct(source.shape, F32),) * 2,
        in_specs=[vmem, pl.BlockSpec(memory_space=pl.ANY), vmem, vmem],
        out_specs=(vmem, vmem),
        scratch_shapes=[
            pltpu.VMEM(links.shape[1:], F32),
            pltpu.VMEM((sites, 2 * comps, sums * comps), BF16),
            pltpu.VMEM((sums * comps, 2 * width), BF16),
            pltpu.VMEM((14, comps, width), F32),
            pltpu.VMEM((8, 2, comps, width), F32),
            pltpu.VMEM((comps, width), F32),
            pltpu.VMEM((SWEEPS + 1, ks + GRAM_ROWS, width), F32),
            pltpu.VMEM((SWEEPS + 1, n, ks + GRAM_ROWS, width), F32),
            pltpu.VMEM((3, GRAM_ROWS, width), F32),
            pltpu.VMEM((3, n, GRAM_ROWS, width), F32),
            pltpu.VMEM((n * sites * ks, width), F32),
            dma((sites,)),
            dma((8, 2)),
            dma((8, 2)),
            dma((SWEEPS + 1,)),
            dma((SWEEPS + 1,)),
            dma((3,)),
            dma((3,)),
        ],
        compiler_params=pltpu.CompilerParams(
            collective_id=0, has_side_effects=True, vmem_limit_bytes=60 * 1024 * 1024
        ),
    )(source, links, prolongator, coarse_inverse)


def solution(mesh):
    return jax.shard_map(
        local,
        mesh=mesh,
        in_specs=(
            P(("groups", "ta"), None, None, None),
            P("ta", None, None, None, None),
            P("ta", None, None, None),
            P("ta", None),
        ),
        out_specs=(P(("groups", "ta"), None, None, None), P(("groups", "ta"), None, None, None)),
        check_vma=False,
    )
```

time: 356 us -> 71.5 us (0.20)
  blocking collectives: 240 us -> 0 us
  matrix products: 79.1 us -> 0 us
  Pallas kernels: 0 us -> 67.5 us
  waiting for transfers between devices: 18.3 us -> 0 us
  starting transfers between devices: 10.4 us -> 0 us
    psum x7 -> x0, blocking collectives: 223 us -> none  [global_pair(): lax.psum((jnp.sum(image * residual, axis=(0, 1, 3)), jnp.sum(image * imag...]
    dot_general x10 -> x0, matrix products: 79.1 us -> none  [the longest x7 78.2 us: operate(): jnp.einsum('tsmab,tsmjb->tsja', links, neighbour_stack(padded), precision...]
    pallas_call x0 -> x1, Pallas kernels: none -> 67.5 us  [local(): pl.pallas_call(functools.partial(kernel, n), out_shape=(jax.ShapeDtypeStr...]
    ppermute x14 -> x0, waiting for transfers between devices: 18.3 us -> none  [the longest x7 13.8 us: padded_2(): lax.ppermute(tail, axis, [(i, (i + 1) % count) for i in range(count)])]
    all_gather x1 -> x0, blocking collectives: 17.9 us -> none  [local(): lax.all_gather(restricted, 'ta', axis=0, tiled=True)]
    ppermute x14 -> x0, starting transfers between devices: 10.4 us -> none  [the longest x7 7.94 us: padded_2(): lax.ppermute(head, axis, [((i + 1) % count, i) for i in range(count)])]
  transfers between devices with their start and end apart: 14 -> 0, of which waited for: 6 -> 0; matrix products, arithmetic and copies ran while one was open for 1% -> 0% of each run, Pallas kernels for 0% -> 0%
where the time goes in v1:
time: 71.5 us; the launch traced here: 71.3 us
  Pallas kernels  67.5 us (94%)
  local copies, waits for them, and re-layouts  3.14 us (4%)
    pallas_call x1, Pallas kernels, local(): pl.pallas_call(functools.partial(kernel, n), out_shape=(jax.ShapeDtypeStr...  67.5 us
    unnamed x2, local copies, waits for them, and re-layouts  3.14 us

profile of v1, /device:TPU:0, one launch (start us, length us, event | category | flops | bytes accessed | tf_op | source)
XLA Modules:
  0.0 71.3 jit_solution(9324388062619747786)
XLA Ops:
  0.6 67.5 %shard_map.59 = (f32[1,4,32,256]{3,2,1,0:T(8,128)}, f32[1,4,32,256]{3,2,1,0:T(8,128)}) custom-call(f32[1,4,32,256]{3,2,1,0:T(8,128)} %source_ref.1, f32[1,4,9,256,256]{4,3,2,1,0:T(8,128)} %links_ref.1, f32[1,4,16,256]{3,2,1,0:T(8,128)} %prol_ref.1, f32[64,1024]{1,0:T(8,128)} %inverse_ref.1), custom_call_target="tpu_custom_call" | custom-call | tf_op jit(solution)/shard_map/pallas_call | solution.py:301
  68.2 1.6 %copy.8 = f32[1,4,32,256]{3,2,1,0:T(8,128)} copy(f32[1,4,32,256]{3,2,1,0:T(8,128)} %get-tuple-element.4) | data formatting | bytes 262144
  69.7 1.6 %copy.9 = f32[1,4,32,256]{3,2,1,0:T(8,128)} copy(f32[1,4,32,256]{3,2,1,0:T(8,128)} %get-tuple-element.5) | data formatting | bytes 262144

commit v2 on v1

--- a/solution.py
+++ b/solution.py
@@ -15,7 +15,7 @@
 HIGHEST = lax.Precision.HIGHEST
 F32 = jnp.float32
 BF16 = jnp.bfloat16
-GRAM_ROWS = 8
+SMALL_ROWS = 2
 
 
 def dot(a, b):
@@ -34,7 +34,11 @@
     lcat,
     weights,
     field,
+    outgoing,
     halo,
+    prol_halo,
+    coarse_out,
+    coarse_halo,
     acc,
     stage,
     gather,
@@ -44,6 +48,8 @@
     link_sem,
     halo_send,
     halo_recv,
+    near_send,
+    near_recv,
     gather_send,
     gather_recv,
     small_send,
@@ -83,32 +89,52 @@
         full = jnp.where(diagonal, dot(prol, v), 0.0)
         return functools.reduce(jnp.add, [full[s * ks : (s + 1) * ks] for s in range(sites)])
 
-    def products(pairs):
-        rows = [jnp.sum(a * b, axis=0, keepdims=True) for a, b in pairs]
-        return jnp.concatenate(rows + [jnp.zeros((GRAM_ROWS - len(rows), width), F32)], axis=0)
-
-    def halo_copies(r, f):
-        out = []
+    def products(pairs, rows=1):
+        packed = []
+        for at in range(0, rows * sites, sites):
+            row = jnp.zeros((1, width), F32)
+            for i, (a, b) in enumerate(pairs[at : at + sites]):
+                row = jnp.where(lane_site == i, over_sites(jnp.sum(a * b, axis=0, keepdims=True)), row)
+            packed.append(row)
+        return packed[0] if rows == 1 else jnp.concatenate(packed, axis=0)
+
+    block = comps // sites
+
+    def send_site(r, s, v):
+        message = jnp.zeros((block, width), F32)
+        for q in range(sites):
+            moved = pltpu.roll(
+                v[q * block : (q + 1) * block], lax.rem(q + sites - s, sites) * rhs, 1
+            )
+            message = jnp.where(lane_site == q, moved, message)
+        outgoing[r, s] = message
         for side, to in ((0, left), (1, right)):
-            out.append(
-                pltpu.make_async_remote_copy(
-                    src_ref=field.at[f],
-                    dst_ref=halo.at[r, side],
-                    send_sem=halo_send.at[r, side],
-                    recv_sem=halo_recv.at[r, side],
-                    device_id={"ta": to},
-                )
+            pltpu.make_async_remote_copy(
+                src_ref=outgoing.at[r, s],
+                dst_ref=halo.at[r, side, s],
+                send_sem=halo_send.at[r, side],
+                recv_sem=halo_recv.at[r, side, s],
+                device_id={"ta": to},
+            ).start()
+
+    def send_field(r, f):
+        def one(s, carry):
+            send_site(r, s, field[f])
+            return carry
+
+        lax.fori_loop(0, sites, one, 0)
+
+    def near(k, src, dst):
+        return [
+            pltpu.make_async_remote_copy(
+                src_ref=src,
+                dst_ref=dst.at[side],
+                send_sem=near_send.at[k, side],
+                recv_sem=near_recv.at[k, side],
+                device_id={"ta": to},
             )
-        return out
-
-    sent = []
-
-    def send_halo(r, f):
-        copies = halo_copies(r, f)
-        for c in copies:
-            c.start()
-        sent.extend(copies)
-        return copies
+            for side, to in ((0, left), (1, right))
+        ]
 
     def exchange(k, value, staged, slots, send_sem, recv_sem):
         staged[k] = value
@@ -151,37 +177,55 @@
         weights[at * comps : (at + 1) * comps, :width] = hi
         weights[at * comps : (at + 1) * comps, width:] = lo
 
-    def multiply(lo_k, hi_k, add):
-        def site(s, carry):
-            p = jnp.dot(
-                lcat[s, :, lo_k * comps : hi_k * comps],
-                weights[lo_k * comps : hi_k * comps],
-                preferred_element_type=F32,
-            )
-            z = p[:comps, :width] + p[:comps, width:] + p[comps:, :width]
-            if add:
-                acc[...] += jnp.where(lane_site == s, z, 0.0)
-            else:
-                acc[...] = jnp.where(lane_site == s, z, acc[...])
-            return carry
-
-        lax.fori_loop(0, sites, site, 0)
-
-    def hop(r, f, shade=None):
+    def product(s, lo_k, hi_k):
+        p = jnp.dot(
+            lcat[s, :, lo_k * comps : hi_k * comps],
+            weights[lo_k * comps : hi_k * comps],
+            preferred_element_type=F32,
+        )
+        return p[:comps, :width] + p[:comps, width:] + p[comps:, :width]
+
+    def inner(f):
         v = field[f]
         load_weights(0, v)
         load_weights(1, pltpu.roll(v, width // 2, 1))
         load_weights(2, jnp.where(even, pltpu.roll(v, width - rhs, 1), pltpu.roll(v, rhs, 1)))
-        multiply(0, INNER_SUMS, False)
-        copies = sent[-2:]
-        for side, c in enumerate(copies):
-            c.wait_recv()
-            load_weights(INNER_SUMS + side, halo[r, side])
-        multiply(INNER_SUMS, len(LINK_SUMS), True)
-        return acc[...]
-
-    def step(r, f, to):
-        field[to] = (1.0 - STEP) * field[f] - STEP * hop(r, f)
+
+        def site(s, carry):
+            acc[...] = jnp.where(lane_site == s, product(s, 0, INNER_SUMS), acc[...])
+            return carry
+
+        lax.fori_loop(0, sites, site, 0)
+
+    def outer(r, f, to, of_field, of_links, send=None):
+        def site(s, carry):
+            if r is not None:
+                for side in range(2):
+                    pltpu.make_async_remote_copy(
+                        src_ref=outgoing.at[r, s],
+                        dst_ref=halo.at[r, side, s],
+                        send_sem=halo_send.at[r, side],
+                        recv_sem=halo_recv.at[r, side, s],
+                        device_id={"ta": left},
+                    ).wait_recv()
+                    m = halo[r, side, s]
+                    load_weights(
+                        INNER_SUMS + side,
+                        jnp.concatenate(
+                            [
+                                pltpu.roll(m, lax.rem(s + sites - q, sites) * rhs, 1)
+                                for q in range(sites)
+                            ],
+                            axis=0,
+                        ),
+                    )
+            new = of_field * field[f] + of_links * (acc[...] + product(s, INNER_SUMS, len(LINK_SUMS)))
+            field[to] = jnp.where(lane_site == s, new, field[to])
+            if send is not None:
+                send_site(send, s, new)
+            return carry
+
+        lax.fori_loop(0, sites, site, 0)
 
     def sweeps(gram):
         c = [jnp.ones((1, width), F32)]
@@ -205,7 +249,10 @@
 
     field[0] = source_ref[0].reshape(width, comps).T
     pl.semaphore_wait(barrier, n - 1)
-    send_halo(0, 0)
+    send_field(0, 0)
+    prol_copies = near(0, prol_ref.at[0], prol_halo)
+    for copy in prol_copies:
+        copy.start()
 
     def prepare(s, carry):
         pltpu.make_async_copy(links_ref.at[0, s], raw.at[s], link_sem.at[s]).wait()
@@ -219,24 +266,28 @@
 
     lax.fori_loop(0, sites, prepare, 0)
     for k in range(SWEEPS + 1):
-        if k:
-            send_halo(k, k)
         value = jnp.concatenate(
             [restrict(field[k]), products([(field[k], field[i]) for i in range(k + 1)])], axis=0
         )
         exchange_large(k, value)
-        step(k, k, k + 1)
+        inner(k)
+        outer(k, k, k + 1, 1.0 - STEP, -STEP, k + 1 if k < SWEEPS else None)
     for k in range(SWEEPS + 1):
         pending[k].wait_recv()
 
-    def total_of(slots, k, at):
+    def total_of(slots, k, at, rows):
         def one(t, total):
-            return total + slots[k, t, at : at + GRAM_ROWS]
-
-        return over_sites(lax.fori_loop(0, n, one, jnp.zeros((GRAM_ROWS, width), F32)))
-
-    grams = [total_of(gather, k, ks) for k in range(SWEEPS + 1)]
-    c, x = sweeps(lambda i, j: grams[max(i, j)][min(i, j) : min(i, j) + 1])
+            return total + slots[k, t, at : at + rows]
+
+        return lax.fori_loop(0, n, one, jnp.zeros((rows, width), F32))
+
+    def unpack(total, i):
+        row = total[i // sites : i // sites + 1]
+        return over_sites(jnp.where(lane_site == i % sites, row, 0.0))
+
+    totals = [total_of(gather, k, ks, 1) for k in range(SWEEPS + 1)]
+    grams = {(k, i): unpack(totals[k], i) for k in range(SWEEPS + 1) for i in range(k + 1)}
+    c, x = sweeps(lambda i, j: grams[max(i, j), min(i, j)])
 
     def spread(t, carry):
         r = functools.reduce(jnp.add, [c[k] * gather[k, t, :ks] for k in range(SWEEPS + 1)])
@@ -248,45 +299,65 @@
 
     lax.fori_loop(0, n, spread, 0)
     coarse = over_sites(dot(inverse_ref[...], rall[...]))
-    field[5] = dot(prol.T, jnp.where(diagonal, coarse, 0.0))
-    send_halo(4, 5)
-    residual = combine(c, range(SWEEPS + 1))
-    field[7] = residual
+    coarse = jnp.where(diagonal, coarse, 0.0)
+    compact = functools.reduce(jnp.add, [coarse[s * ks : (s + 1) * ks] for s in range(sites)])
+    coarse_out[...] = compact
+    coarse_copies = near(1, coarse_out, coarse_halo)
+    for copy in coarse_copies:
+        copy.start()
+    field[5] = dot(prol.T, coarse)
+    inner(5)
+    field[7] = combine(c, range(SWEEPS + 1))
     field[8] = combine(c, range(1, SWEEPS + 2))
     field[9] = combine(x, range(SWEEPS))
-    field[6] = field[5] + hop(4, 5)
-    send_halo(5, 6)
-    exchange_small(0, products([(field[6], field[7]), (field[6], field[6])]))
-    after = (1.0 - STEP) * field[6] - STEP * hop(5, 6)
+    for side in range(2):
+        prol_copies[side].wait_recv()
+        coarse_copies[side].wait_recv()
+        there = jnp.where(diagonal, jnp.concatenate([coarse_halo[side]] * sites, axis=0), 0.0)
+        vectors = prol_halo[side].reshape(sites * ks, comps)
+        load_weights(INNER_SUMS + side, dot(vectors.T, there))
+    outer(None, 5, 6, 1.0, 1.0, 4)
+    exchange_small(0, products([(field[6], field[7]), (field[6], field[6])], SMALL_ROWS))
+    inner(6)
+    outer(4, 6, 14, 1.0 - STEP, -STEP)
     pending[-1].wait_recv()
-    pair = total_of(small, 0, 0)
-    g = pair[0:1] / pair[1:2]
-
-    field[11] = field[8] - g * after
-    send_halo(6, 11)
+    pair = total_of(small, 0, 0, SMALL_ROWS)
+    g = unpack(pair, 0) / unpack(pair, 1)
+
+    field[11] = field[8] - g * field[14]
+    send_field(5, 11)
     field[10] = field[7] - g * field[6]
     field[9] = field[9] + g * field[5]
-    step(6, 11, 12)
-    send_halo(7, 12)
+    inner(11)
+    outer(5, 11, 12, 1.0 - STEP, -STEP, 6)
     early = [(i, j) for i in range(3) for j in range(i + 1)]
     late = [(3, j) for j in range(4)]
-    exchange_small(1, products([(field[10 + i], field[10 + j]) for i, j in early]))
-    step(7, 12, 13)
-    exchange_small(2, products([(field[10 + i], field[10 + j]) for i, j in late]))
+    exchange_small(1, products([(field[10 + i], field[10 + j]) for i, j in early], SMALL_ROWS))
+    inner(12)
+    outer(6, 12, 13, 1.0 - STEP, -STEP)
+    exchange_small(2, products([(field[10 + i], field[10 + j]) for i, j in late], SMALL_ROWS))
     pending[-2].wait_recv()
     pending[-1].wait_recv()
-    sums = [total_of(small, 1, 0), total_of(small, 2, 0)]
+    sums = [total_of(small, 1, 0, SMALL_ROWS), total_of(small, 2, 0, SMALL_ROWS)]
+    grams_after = {pair: unpack(sums[0], early.index(pair)) for pair in early}
+    grams_after.update({pair: unpack(sums[1], late.index(pair)) for pair in late})
 
     def gram(i, j):
-        pair = (max(i, j), min(i, j))
-        which = 0 if pair in early else 1
-        row = (early, late)[which].index(pair)
-        return sums[which][row : row + 1]
+        return grams_after[max(i, j), min(i, j)]
 
     c, x = sweeps(gram)
     residual_ref[0] = combine(c, range(10, 14)).T.reshape(sites, rhs, comps)
     solution_ref[0] = (field[9] + combine(x, range(10, 13))).T.reshape(sites, rhs, comps)
-    for copy in sent + pending:
+    for r in range(halo.shape[0]):
+        for side in range(2):
+            pltpu.make_async_remote_copy(
+                src_ref=outgoing.at[r],
+                dst_ref=halo.at[r, side],
+                send_sem=halo_send.at[r, side],
+                recv_sem=halo_recv.at[r, side, 0],
+                device_id={"ta": left},
+            ).wait_send()
+    for copy in pending + prol_copies + coarse_copies:
         copy.wait_send()
 
 
@@ -307,17 +378,23 @@
             pltpu.VMEM(links.shape[1:], F32),
             pltpu.VMEM((sites, 2 * comps, sums * comps), BF16),
             pltpu.VMEM((sums * comps, 2 * width), BF16),
-            pltpu.VMEM((14, comps, width), F32),
-            pltpu.VMEM((8, 2, comps, width), F32),
+            pltpu.VMEM((15, comps, width), F32),
+            pltpu.VMEM((7, sites, comps // sites, width), F32),
+            pltpu.VMEM((7, 2, sites, comps // sites, width), F32),
+            pltpu.VMEM((2, *prolongator.shape[1:]), F32),
+            pltpu.VMEM((ks, width), F32),
+            pltpu.VMEM((2, ks, width), F32),
             pltpu.VMEM((comps, width), F32),
-            pltpu.VMEM((SWEEPS + 1, ks + GRAM_ROWS, width), F32),
-            pltpu.VMEM((SWEEPS + 1, n, ks + GRAM_ROWS, width), F32),
-            pltpu.VMEM((3, GRAM_ROWS, width), F32),
-            pltpu.VMEM((3, n, GRAM_ROWS, width), F32),
+            pltpu.VMEM((SWEEPS + 1, ks + 1, width), F32),
+            pltpu.VMEM((SWEEPS + 1, n, ks + 1, width), F32),
+            pltpu.VMEM((3, SMALL_ROWS, width), F32),
+            pltpu.VMEM((3, n, SMALL_ROWS, width), F32),
             pltpu.VMEM((n * sites * ks, width), F32),
             dma((sites,)),
-            dma((8, 2)),
-            dma((8, 2)),
+            dma((7, 2)),
+            dma((7, 2, sites)),
+            dma((2, 2)),
+            dma((2, 2)),
             dma((SWEEPS + 1,)),
             dma((SWEEPS + 1,)),
             dma((3,)),

time: 71.5 us -> 61.8 us (0.86)
  Pallas kernels: 67.5 us -> 57.9 us
    pallas_call x1, Pallas kernels: 67.5 us -> 57.9 us  [local(): pl.pallas_call(functools.partial(kernel, n), out_shape=(jax.ShapeDtypeStr...]
where the time goes in v2:
time: 61.8 us; the launch traced here: 61.6 us
  Pallas kernels  57.9 us (94%)
  local copies, waits for them, and re-layouts  3.14 us (5%)
  between operations  0.64 us (1%)
    pallas_call x1, Pallas kernels, local(): pl.pallas_call(functools.partial(kernel, n), out_shape=(jax.ShapeDtypeStr...  57.9 us
    unnamed x2, local copies, waits for them, and re-layouts  3.14 us

profile of v2, /device:TPU:0, one launch (start us, length us, event | category | flops | bytes accessed | tf_op | source)
XLA Modules:
  0.0 61.6 jit_solution(10642214774874510533)
XLA Ops:
  0.6 57.9 %shard_map.59 = (f32[1,4,32,256]{3,2,1,0:T(8,128)}, f32[1,4,32,256]{3,2,1,0:T(8,128)}) custom-call(f32[1,4,32,256]{3,2,1,0:T(8,128)} %source_ref.1, f32[1,4,9,256,256]{4,3,2,1,0:T(8,128)} %links_ref.1, f32[1,4,16,256]{3,2,1,0:T(8,128)} %prol_ref.1, f32[64,1024]{1,0:T(8,128)} %inverse_ref.1), custom_call_target="tpu_custom_call" | custom-call | tf_op jit(solution)/shard_map/pallas_call | solution.py:372
  58.5 1.6 %copy.8 = f32[1,4,32,256]{3,2,1,0:T(8,128)} copy(f32[1,4,32,256]{3,2,1,0:T(8,128)} %get-tuple-element.4) | data formatting | bytes 262144
  60.1 1.6 %copy.9 = f32[1,4,32,256]{3,2,1,0:T(8,128)} copy(f32[1,4,32,256]{3,2,1,0:T(8,128)} %get-tuple-element.5) | data formatting | bytes 262144

commit v3 on v2

--- a/solution.py
+++ b/solution.py
@@ -85,8 +85,20 @@
     row_site = lax.broadcasted_iota(jnp.int32, (sites * ks, width), 0) // ks
     diagonal = row_site == lax.broadcasted_iota(jnp.int32, (sites * ks, width), 1) // rhs
 
-    def restrict(v):
-        full = jnp.where(diagonal, dot(prol, v), 0.0)
+    def two_parts(a):
+        hi = a.astype(BF16)
+        return hi, (a - hi.astype(F32)).astype(BF16)
+
+    prol_parts = jnp.concatenate(two_parts(prol), axis=0)
+    inverse_parts = jnp.concatenate(two_parts(inverse_ref[...]), axis=0)
+
+    def dot_parts(a, b):
+        p = jnp.dot(a, b, preferred_element_type=F32)
+        rows = a.shape[0] // 2
+        return p[:rows, :width] + p[:rows, width:] + p[rows:, :width]
+
+    def restrict():
+        full = jnp.where(diagonal, dot_parts(prol_parts, weights[:comps]), 0.0)
         return functools.reduce(jnp.add, [full[s * ks : (s + 1) * ks] for s in range(sites)])
 
     def products(pairs, rows=1):
@@ -178,24 +190,23 @@
         weights[at * comps : (at + 1) * comps, width:] = lo
 
     def product(s, lo_k, hi_k):
-        p = jnp.dot(
-            lcat[s, :, lo_k * comps : hi_k * comps],
-            weights[lo_k * comps : hi_k * comps],
-            preferred_element_type=F32,
-        )
-        return p[:comps, :width] + p[:comps, width:] + p[comps:, :width]
-
-    def inner(f):
+        k = slice(lo_k * comps, hi_k * comps)
+        p = jnp.dot(lcat[s, :comps, k], weights[k], preferred_element_type=F32)
+        q = jnp.dot(lcat[s, comps:, k], weights[k, :width], preferred_element_type=F32)
+        return p[:, :width] + p[:, width:] + q
+
+    def load_inner(f):
         v = field[f]
         load_weights(0, v)
         load_weights(1, pltpu.roll(v, width // 2, 1))
         load_weights(2, jnp.where(even, pltpu.roll(v, width - rhs, 1), pltpu.roll(v, rhs, 1)))
 
+    def inner():
         def site(s, carry):
             acc[...] = jnp.where(lane_site == s, product(s, 0, INNER_SUMS), acc[...])
             return carry
 
-        lax.fori_loop(0, sites, site, 0)
+        lax.fori_loop(0, sites, site, 0, unroll=True)
 
     def outer(r, f, to, of_field, of_links, send=None):
         def site(s, carry):
@@ -266,11 +277,12 @@
 
     lax.fori_loop(0, sites, prepare, 0)
     for k in range(SWEEPS + 1):
+        load_inner(k)
         value = jnp.concatenate(
-            [restrict(field[k]), products([(field[k], field[i]) for i in range(k + 1)])], axis=0
+            [restrict(), products([(field[k], field[i]) for i in range(k + 1)])], axis=0
         )
         exchange_large(k, value)
-        inner(k)
+        inner()
         outer(k, k, k + 1, 1.0 - STEP, -STEP, k + 1 if k < SWEEPS else None)
     for k in range(SWEEPS + 1):
         pending[k].wait_recv()
@@ -292,13 +304,14 @@
     def spread(t, carry):
         r = functools.reduce(jnp.add, [c[k] * gather[k, t, :ks] for k in range(SWEEPS + 1)])
         for s in range(sites):
-            rall[pl.ds(pl.multiple_of((t * sites + s) * ks, ks), ks)] = jnp.where(
-                lane_site == s, r, 0.0
-            )
+            hi, lo = two_parts(jnp.where(lane_site == s, r, 0.0))
+            at = pl.ds(pl.multiple_of((t * sites + s) * ks, ks), ks)
+            rall[at, :width] = hi
+            rall[at, width:] = lo
         return carry
 
     lax.fori_loop(0, n, spread, 0)
-    coarse = over_sites(dot(inverse_ref[...], rall[...]))
+    coarse = over_sites(dot_parts(inverse_parts, rall[...]))
     coarse = jnp.where(diagonal, coarse, 0.0)
     compact = functools.reduce(jnp.add, [coarse[s * ks : (s + 1) * ks] for s in range(sites)])
     coarse_out[...] = compact
@@ -306,7 +319,8 @@
     for copy in coarse_copies:
         copy.start()
     field[5] = dot(prol.T, coarse)
-    inner(5)
+    load_inner(5)
+    inner()
     field[7] = combine(c, range(SWEEPS + 1))
     field[8] = combine(c, range(1, SWEEPS + 2))
     field[9] = combine(x, range(SWEEPS))
@@ -318,7 +332,8 @@
         load_weights(INNER_SUMS + side, dot(vectors.T, there))
     outer(None, 5, 6, 1.0, 1.0, 4)
     exchange_small(0, products([(field[6], field[7]), (field[6], field[6])], SMALL_ROWS))
-    inner(6)
+    load_inner(6)
+    inner()
     outer(4, 6, 14, 1.0 - STEP, -STEP)
     pending[-1].wait_recv()
     pair = total_of(small, 0, 0, SMALL_ROWS)
@@ -328,12 +343,14 @@
     send_field(5, 11)
     field[10] = field[7] - g * field[6]
     field[9] = field[9] + g * field[5]
-    inner(11)
+    load_inner(11)
+    inner()
     outer(5, 11, 12, 1.0 - STEP, -STEP, 6)
     early = [(i, j) for i in range(3) for j in range(i + 1)]
     late = [(3, j) for j in range(4)]
     exchange_small(1, products([(field[10 + i], field[10 + j]) for i, j in early], SMALL_ROWS))
-    inner(12)
+    load_inner(12)
+    inner()
     outer(6, 12, 13, 1.0 - STEP, -STEP)
     exchange_small(2, products([(field[10 + i], field[10 + j]) for i, j in late], SMALL_ROWS))
     pending[-2].wait_recv()
@@ -346,8 +363,8 @@
         return grams_after[max(i, j), min(i, j)]
 
     c, x = sweeps(gram)
-    residual_ref[0] = combine(c, range(10, 14)).T.reshape(sites, rhs, comps)
-    solution_ref[0] = (field[9] + combine(x, range(10, 13))).T.reshape(sites, rhs, comps)
+    residual_ref[...] = combine(c, range(10, 14))
+    solution_ref[...] = field[9] + combine(x, range(10, 13))
     for r in range(halo.shape[0]):
         for side in range(2):
             pltpu.make_async_remote_copy(
@@ -361,6 +378,11 @@
         copy.wait_send()
 
 
+def turn(*refs):
+    for column, row in zip(refs[:2], refs[2:]):
+        row[0] = column[...].T.reshape(row.shape[1:])
+
+
 def local(source, links, prolongator, coarse_inverse):
     n = lax.axis_size("ta")
     _, sites, rhs, comps = source.shape
@@ -369,9 +391,9 @@
     sums = len(LINK_SUMS)
     vmem = pl.BlockSpec(memory_space=pltpu.VMEM)
     dma = pltpu.SemaphoreType.DMA
-    return pl.pallas_call(
+    columns = pl.pallas_call(
         functools.partial(kernel, n),
-        out_shape=(jax.ShapeDtypeStruct(source.shape, F32),) * 2,
+        out_shape=(jax.ShapeDtypeStruct((comps, width), F32),) * 2,
         in_specs=[vmem, pl.BlockSpec(memory_space=pl.ANY), vmem, vmem],
         out_specs=(vmem, vmem),
         scratch_shapes=[
@@ -389,7 +411,7 @@
             pltpu.VMEM((SWEEPS + 1, n, ks + 1, width), F32),
             pltpu.VMEM((3, SMALL_ROWS, width), F32),
             pltpu.VMEM((3, n, SMALL_ROWS, width), F32),
-            pltpu.VMEM((n * sites * ks, width), F32),
+            pltpu.VMEM((n * sites * ks, 2 * width), BF16),
             dma((sites,)),
             dma((7, 2)),
             dma((7, 2, sites)),
@@ -404,6 +426,12 @@
             collective_id=0, has_side_effects=True, vmem_limit_bytes=60 * 1024 * 1024
         ),
     )(source, links, prolongator, coarse_inverse)
+    return pl.pallas_call(
+        turn,
+        out_shape=(jax.ShapeDtypeStruct(source.shape, F32),) * 2,
+        in_specs=[vmem, vmem],
+        out_specs=(vmem, vmem),
+    )(*columns)
 
 
 def solution(mesh):

time: 61.8 us -> 59.3 us (0.960)
  local copies, waits for them, and re-layouts: 3.14 us -> 0 us
    unnamed x2 -> x0, local copies, waits for them, and re-layouts: 3.14 us -> none
    pallas_call x0 -> x1, Pallas kernels: none -> 1.77 us  [local(): pl.pallas_call(turn, out_shape=(jax.ShapeDtypeStruct(source.shape, F32),)...]
    pallas_call x1, Pallas kernels: 57.9 us -> 56.8 us  [local(): pl.pallas_call(functools.partial(kernel, n), out_shape=(jax.ShapeDtypeStr...]
where the time goes in v3:
time: 59.3 us; the launch traced here: 59.2 us
  Pallas kernels  58.5 us (99%)
  between operations  0.64 us (1%)
    pallas_call x1, Pallas kernels, local(): pl.pallas_call(functools.partial(kernel, n), out_shape=(jax.ShapeDtypeStr...  56.8 us
    pallas_call x1, Pallas kernels, local(): pl.pallas_call(turn, out_shape=(jax.ShapeDtypeStruct(source.shape, F32),)...  1.77 us

profile of v3, /device:TPU:0, one launch (start us, length us, event | category | flops | bytes accessed | tf_op | source)
XLA Modules:
  0.0 59.2 jit_solution(13170770401868453242)
XLA Ops:
  0.6 56.8 %shard_map.59 = (f32[256,128]{1,0:T(8,128)}, f32[256,128]{1,0:T(8,128)}) custom-call(f32[1,4,32,256]{3,2,1,0:T(8,128)} %source_ref.1, f32[1,4,9,256,256]{4,3,2,1,0:T(8,128)} %links_ref.1, f32[1,4,16,256]{3,2,1,0:T(8,128)} %prol_ref.1, f32[64,1024]{1,0:T(8,128)} %inverse_ref.1), custom_call_target="tpu_custom_call" | custom-call | tf_op jit(solution)/shard_map/pallas_call | solution.py:394
  57.4 1.8 %shard_map.60 = (f32[1,4,32,256]{3,2,1,0:T(8,128)}, f32[1,4,32,256]{3,2,1,0:T(8,128)}) custom-call(f32[256,128]{1,0:T(8,128)} %get-tuple-element.4.refs_0_, f32[256,128]{1,0:T(8,128)} %get-tuple-element.5.refs_1_), custom_call_target="tpu_custom_call" | custom-call | tf_op jit(solution)/shard_map/pallas_call | solution.py:429
